TPU v7x, 512 devices: a whole 4x4x16 slice. The times are simulated.
512 devices in a mesh: dp: 32 (over z, core), seq: 16 (over y, x).
Axes of the slice: x: 4, y: 4, z: 16, core: 2. Of those that a mesh axis runs over, the one named last changes fastest.
Arguments:
- features: bfloat16 [32, 3072, 1024], P('dp', 'seq'), may hold values from -18 to 18
- qkv_weight: bfloat16 [1024, 3072], P('dp'), may hold values from -1 to 1
- cotangent: bfloat16 [32, 3072, 1024], P('dp', 'seq'), may hold values from -6 to 6
- node_order: int32 [32, 3072], P('dp'), may hold values from 0 to 3071, as said below
- blocks: int32 [32, 48, 8], P('dp'), may hold values from 0 to 47, as said below
- counts: int32 [32, 48], P('dp'), may hold values from 1 to 8, as said below
Outputs:
- attended: bfloat16 [32, 3072, 1024], P('dp', 'seq')
- grad_features: bfloat16 [32, 3072, 1024], P('dp', 'seq')
- grad_weight: float32 [1024, 3072], P('dp', 'seq')
Inputs may be any that keep to these rules, and one draw needn't show every extreme that they name: Every row of node_order lists each node of the subgraph once. blocks[g, c, 0] is c, and the 8 entries of a row are distinct clusters; slots at or beyond counts[g, c] are unused. `counts`: every subgraph has a cluster with all 8 slots live.
All inputs are finite; a program needn't handle non-finite values.
Results may differ from a plain program's by a relative error of at most 0.03.
Values may be sent and summed in bfloat16 or wider, within the bound.
No kernel may reach another device: no remote copies, remote signals or barrier semaphores. Data moves between devices by JAX's collectives and lax.ppermute only.
A program may use at most 128 MiB of HBM per device.

v0:
```python
import math
import jax
import jax.numpy as jnp
from jax import lax
from jax.sharding import PartitionSpec as P

HEADS = 16
HD = 64


def attend(query, key_in, value, grad_out, blocks, counts):
    cluster_count, slot_count = blocks.shape
    node_count, head_width = query.shape
    block_rows = node_count // cluster_count
    in_group = math.gcd(cluster_count, 8)
    runs_total = cluster_count // in_group
    score_scale = 1.0 / math.sqrt(head_width)
    key_blocks = key_in.reshape(cluster_count, block_rows, head_width)
    value_blocks = value.reshape(cluster_count, block_rows, head_width)
    inputs_all = (
        query.reshape(runs_total, in_group, block_rows, head_width),
        grad_out.reshape(runs_total, in_group, block_rows, head_width),
        blocks.reshape(runs_total, in_group, slot_count),
        counts.reshape(runs_total, in_group),
    )

    def group_step(totals, inputs_now):
        grad_key, grad_value = totals
        query_block, grad_block, block_ids, live_count = inputs_now
        key_rows = key_blocks[block_ids].reshape(in_group, slot_count * block_rows, head_width)
        value_rows = value_blocks[block_ids].reshape(in_group, slot_count * block_rows, head_width)
        is_live = jnp.repeat(
            jnp.arange(slot_count)[None, :] < live_count[:, None], block_rows, axis=1
        )[:, None, :]
        scores = (
            jnp.einsum("cqe,cke->cqk", query_block, key_rows, preferred_element_type=jnp.float32)
            * score_scale
        )
        scores = jnp.where(is_live, scores, -1e30)
        row_max = jnp.max(scores, axis=-1, keepdims=True)
        raw_weights = jnp.where(is_live, jnp.exp(scores - row_max), 0.0)
        attn_weights = raw_weights / jnp.sum(raw_weights, axis=-1, keepdims=True)
        attn_low = attn_weights.astype(jnp.bfloat16)
        output_blk = jnp.einsum(
            "cqk,cke->cqe", attn_low, value_rows, preferred_element_type=jnp.float32
        ).astype(jnp.bfloat16)
        grad_weights = jnp.einsum(
            "cqe,cke->cqk", grad_block, value_rows, preferred_element_type=jnp.float32
        )
        row_dot = jnp.sum(attn_weights * grad_weights, axis=-1, keepdims=True)
        grad_scores = (attn_weights * (grad_weights - row_dot) * score_scale).astype(jnp.bfloat16)
        grad_query = jnp.einsum(
            "cqk,cke->cqe", grad_scores, key_rows, preferred_element_type=jnp.float32
        ).astype(jnp.bfloat16)
        key_terms = jnp.einsum(
            "cqk,cqe->cke", grad_scores, query_block, preferred_element_type=jnp.float32
        )
        value_terms = jnp.einsum(
            "cqk,cqe->cke", attn_low, grad_block, preferred_element_type=jnp.float32
        )
        grad_key = grad_key.at[block_ids].add(
            key_terms.reshape(in_group, slot_count, block_rows, head_width)
        )
        grad_value = grad_value.at[block_ids].add(
            value_terms.reshape(in_group, slot_count, block_rows, head_width)
        )
        return ((grad_key, grad_value), (output_blk, grad_query))

    empty_sum = jnp.zeros((cluster_count, block_rows, head_width), jnp.float32)
    (grad_key, grad_value), (output_all, grad_query) = lax.scan(
        group_step, (empty_sum, empty_sum), inputs_all
    )
    return (
        output_all.reshape(node_count, head_width),
        grad_query.reshape(node_count, head_width),
        grad_key.reshape(node_count, head_width).astype(jnp.bfloat16),
        grad_value.reshape(node_count, head_width).astype(jnp.bfloat16),
    )


def per_device(features, qkv_weight, cotangent, node_order, blocks, counts):
    local_rows = features.shape[1]
    model_width = features.shape[2]
    heads_local = HEADS // lax.axis_size("seq")
    three_width = 3 * HD
    node_feats = features[0]
    cot_heads = cotangent[0].reshape(local_rows, HEADS, HD)
    weights_all = lax.all_gather(qkv_weight, "dp", axis=0, tiled=True)
    node_all = lax.all_gather(node_feats, "seq", axis=0, tiled=True)
    node_count = node_all.shape[0]
    projected = jnp.dot(node_feats, weights_all, preferred_element_type=jnp.float32).astype(
        jnp.bfloat16
    )
    projected = projected.reshape(local_rows, HEADS, three_width)
    head_qkv, head_cot = (
        lax.all_to_all(projected, "seq", split_axis=1, concat_axis=0, tiled=True),
        lax.all_to_all(cot_heads, "seq", split_axis=1, concat_axis=0, tiled=True),
    )
    graph_order = node_order[0]
    inverse = (
        jnp.zeros((node_count,), jnp.int32)
        .at[graph_order]
        .set(jnp.arange(node_count, dtype=jnp.int32))
    )
    sorted_qkv = head_qkv[graph_order]
    sorted_cot = head_cot[graph_order]
    output_all, grad_query, grad_key, grad_value = jax.vmap(
        attend, in_axes=(1, 1, 1, 1, None, None), out_axes=1
    )(
        sorted_qkv[:, :, :HD],
        sorted_qkv[:, :, HD : 2 * HD],
        sorted_qkv[:, :, 2 * HD :],
        sorted_cot,
        blocks[0],
        counts[0],
    )
    grad_heads = jnp.concatenate([grad_query, grad_key, grad_value], axis=-1)[inverse]
    output_nodes = output_all[inverse]
    output_back, grad_back = (
        lax.all_to_all(output_nodes, "seq", split_axis=0, concat_axis=1, tiled=True),
        lax.all_to_all(grad_heads, "seq", split_axis=0, concat_axis=1, tiled=True),
    )
    attended = output_back.reshape(1, local_rows, model_width)
    grad_local = grad_back.reshape(local_rows, 3 * model_width)
    grad_feats = lax.dot_general(
        grad_local, weights_all, (((1,), (1,)), ((), ())), preferred_element_type=jnp.float32
    )
    grad_features = grad_feats.astype(jnp.bfloat16).reshape(1, local_rows, model_width)
    head_grads = grad_heads.reshape(node_count, heads_local * three_width)
    grad_weight = lax.psum_scatter(
        lax.dot_general(
            node_all, head_grads, (((0,), (0,)), ((), ())), preferred_element_type=jnp.float32
        ).astype(jnp.bfloat16),
        "dp",
        scatter_dimension=0,
        tiled=True,
    ).astype(jnp.float32)
    return (attended, grad_features, grad_weight)


def solution(mesh):
    return jax.shard_map(
        per_device,
        mesh=mesh,
        in_specs=(
            P("dp", "seq", None),
            P("dp", None),
            P("dp", "seq", None),
            P("dp", None),
            P("dp", None, None),
            P("dp", None),
        ),
        out_specs=(P("dp", "seq", None), P("dp", "seq", None), P("dp", "seq")),
        check_vma=False,
    )
```

profile of v0, /device:TPU:8, one launch (start us, length us, event | category | flops | bytes accessed | tf_op | source)
XLA Modules:
  0.0 628.1 jit_solution(6024842970168261089)
XLA Ops:
  9.9 9.2 %all-to-all-start.1 = ((bf16[192,16,64]{0,2,1:T(8,128)(2,1)}), bf16[192,16,64]{0,2,1:T(8,128)(2,1)S(1)}, u32[]{:S(2)}, u32[]{:S(2)}) async-start(bf16[192,16,64]{0,2,1:T(8,128)(2,1)} %bitcast.27), calls=%async_computation.1 | async-start | bytes 1048576 | tf_op jit(solution)/shard_map/all_to_all | solution.py:97
  21.2 70.2 %all-gather.4.cloned.1.call-done = bf16[1024,3072]{1,0:T(8,128)(2,1)} async-done(((bf16[32,3072]{1,0:T(8,128)(2,1)}), bf16[1024,3072]{1,0:T(8,128)(2,1)}) %all-gather.4.cloned.1.call-update) | async-done | bytes 6291472 | tf_op jit(solution)/shard_map/all_gather | solution.py:88
  101.5 7.4 %all-to-all-start = ((bf16[192,16,192]{2,0,1:T(8,128)(2,1)}), bf16[192,16,192]{2,0,1:T(8,128)(2,1)S(1)}, u32[]{:S(2)}, u32[]{:S(2)}) async-start(bf16[192,16,192]{2,0,1:T(8,128)(2,1)} %copy.93), calls=%async_computation | async-start | bytes 3145728 | tf_op jit(solution)/shard_map/all_to_all | solution.py:96
  108.9 12.0 %scatter_custom_fusion.2 = s32[3072]{0:T(1024)S(1)} fusion(s32[3072]{0:T(1024)S(1)} %bitcast.182, s32[3072]{0:T(1024)S(1)} %iota.7, s32[]{:T(128)} %copy.139), kind=kCustom, calls=%fused_computation.71 | custom fusion | bytes 12292 | tf_op jit(solution)/shard_map/scatter | solution.py:103
  121.3 11.4 %gather_fusion.3 = bf16[3072,64]{1,0:T(8,128)(2,1)} fusion(bf16[3072,64]{1,0:T(8,128)(2,1)S(1)} %bitcast.161, s32[3072]{0:T(1024)S(1)} %broadcast_clamp_fusion), kind=kCustom, calls=%fused_computation.3 | custom fusion | bytes 798720 | tf_op jit(solution)/shard_map/gather | solution.py:106
  137.2 11.1 %gather_fusion.2 = bf16[3072,192]{1,0:T(8,128)(2,1)S(1)} fusion(bf16[3072,192]{1,0:T(8,128)(2,1)S(1)} %bitcast.152, s32[3072]{0:T(1024)S(1)} %broadcast_clamp_fusion), kind=kCustom, calls=%fused_computation.2 | custom fusion | bytes 2371584 | tf_op jit(solution)/shard_map/gather | solution.py:105
  150.4 286.3 %while.16 = (s32[]{:T(128)}, f32[1,48,64,64]{3,2,1,0:T(8,128)S(1)}, f32[1,48,64,64]{3,2,1,0:T(8,128)S(1)}, bf16[6,1,8,64,64]{4,3,2,1,0:T(8,128)(2,1)}, bf16[6,1,...) while((s32[]{:T(128)}, f32[1,48,64,64]{3,2,1,0:T(8,128)S(1)}, ...), condition=%wide.region_6.7_spmd, body=%wide.region_0.6_spmd.sunk | while | flops 209000192 | bytes 36499064 | solution.py:70
  173.6 7.0 %scatter_fusion.1 = f32[48,64,64]{2,1,0:T(8,128)S(1)} fusion(f32[48,64,64]{2,1,0:T(8,128)S(1)} %bitcast.155, s32[64]{0:T(128)S(1)} %reshape.343, f32[64,64,64]{2,1,0:T(8,128)} %bitcast.163), kind=kCustom, calls=%fused_computation.7.clone.1 | custom fusion | flops 262144 | bytes 3145984 | tf_op jit(solution)/shard_map/vmap()/while/body/eval_jaxpr/scatter-add | solution.py:64
  180.6 7.0 %fusion.110 = f32[8,512,64]{2,1,0:T(8,128)} fusion(f32[8,64,512]{2,1,0:T(8,128)} %fusion.106, bf16[6,1,8,64,64]{4,3,2,1,0:T(8,128)(2,1)} %get-tuple-element.266, s32[]{:T(128)} %get-tuple-element.247, f32[8,64,512]{2,1,0:T(8,128)} %get-tuple-element.233, f32[8,64]{1,0:T(8,128)S(1)} %get-tuple-element.234), kind=kOutput, calls=%fused_computation.26.clone.1 | convolution fusion | flops 35390464 | bytes 5382656 | tf_op jit(solution)/shard_map/vmap()/while/body/eval_jaxpr/reshape | solution.py:62
  187.7 7.0 %scatter_fusion = f32[48,64,64]{2,1,0:T(8,128)S(1)} fusion(f32[48,64,64]{2,1,0:T(8,128)S(1)} %bitcast.153, s32[64]{0:T(128)S(1)} %reshape.343, f32[64,64,64]{2,1,0:T(8,128)} %bitcast.162), kind=kCustom, calls=%fused_computation.6.clone.1 | custom fusion | flops 262144 | bytes 3145984 | tf_op jit(solution)/shard_map/vmap()/while/body/eval_jaxpr/scatter-add | solution.py:61
  221.3 7.0 %scatter_fusion.1 = f32[48,64,64]{2,1,0:T(8,128)S(1)} fusion(f32[48,64,64]{2,1,0:T(8,128)S(1)} %bitcast.155, s32[64]{0:T(128)S(1)} %reshape.343, f32[64,64,64]{2,1,0:T(8,128)} %bitcast.163), kind=kCustom, calls=%fused_computation.7.clone.1 | custom fusion | flops 262144 | bytes 3145984 | tf_op jit(solution)/shard_map/vmap()/while/body/eval_jaxpr/scatter-add | solution.py:64
  228.3 7.0 %fusion.110 = f32[8,512,64]{2,1,0:T(8,128)} fusion(f32[8,64,512]{2,1,0:T(8,128)} %fusion.106, bf16[6,1,8,64,64]{4,3,2,1,0:T(8,128)(2,1)} %get-tuple-element.266, s32[]{:T(128)} %get-tuple-element.247, f32[8,64,512]{2,1,0:T(8,128)} %get-tuple-element.233, f32[8,64]{1,0:T(8,128)S(1)} %get-tuple-element.234), kind=kOutput, calls=%fused_computation.26.clone.1 | convolution fusion | flops 35390464 | bytes 5382656 | tf_op jit(solution)/shard_map/vmap()/while/body/eval_jaxpr/reshape | solution.py:62
  235.4 7.0 %scatter_fusion = f32[48,64,64]{2,1,0:T(8,128)S(1)} fusion(f32[48,64,64]{2,1,0:T(8,128)S(1)} %bitcast.153, s32[64]{0:T(128)S(1)} %reshape.343, f32[64,64,64]{2,1,0:T(8,128)} %bitcast.162), kind=kCustom, calls=%fused_computation.6.clone.1 | custom fusion | flops 262144 | bytes 3145984 | tf_op jit(solution)/shard_map/vmap()/while/body/eval_jaxpr/scatter-add | solution.py:61
  269.0 7.0 %scatter_fusion.1 = f32[48,64,64]{2,1,0:T(8,128)S(1)} fusion(f32[48,64,64]{2,1,0:T(8,128)S(1)} %bitcast.155, s32[64]{0:T(128)S(1)} %reshape.343, f32[64,64,64]{2,1,0:T(8,128)} %bitcast.163), kind=kCustom, calls=%fused_computation.7.clone.1 | custom fusion | flops 262144 | bytes 3145984 | tf_op jit(solution)/shard_map/vmap()/while/body/eval_jaxpr/scatter-add | solution.py:64
  276.0 7.0 %fusion.110 = f32[8,512,64]{2,1,0:T(8,128)} fusion(f32[8,64,512]{2,1,0:T(8,128)} %fusion.106, bf16[6,1,8,64,64]{4,3,2,1,0:T(8,128)(2,1)} %get-tuple-element.266, s32[]{:T(128)} %get-tuple-element.247, f32[8,64,512]{2,1,0:T(8,128)} %get-tuple-element.233, f32[8,64]{1,0:T(8,128)S(1)} %get-tuple-element.234), kind=kOutput, calls=%fused_computation.26.clone.1 | convolution fusion | flops 35390464 | bytes 5382656 | tf_op jit(solution)/shard_map/vmap()/while/body/eval_jaxpr/reshape | solution.py:62
  283.1 7.0 %scatter_fusion = f32[48,64,64]{2,1,0:T(8,128)S(1)} fusion(f32[48,64,64]{2,1,0:T(8,128)S(1)} %bitcast.153, s32[64]{0:T(128)S(1)} %reshape.343, f32[64,64,64]{2,1,0:T(8,128)} %bitcast.162), kind=kCustom, calls=%fused_computation.6.clone.1 | custom fusion | flops 262144 | bytes 3145984 | tf_op jit(solution)/shard_map/vmap()/while/body/eval_jaxpr/scatter-add | solution.py:61
  316.7 7.0 %scatter_fusion.1 = f32[48,64,64]{2,1,0:T(8,128)S(1)} fusion(f32[48,64,64]{2,1,0:T(8,128)S(1)} %bitcast.155, s32[64]{0:T(128)S(1)} %reshape.343, f32[64,64,64]{2,1,0:T(8,128)} %bitcast.163), kind=kCustom, calls=%fused_computation.7.clone.1 | custom fusion | flops 262144 | bytes 3145984 | tf_op jit(solution)/shard_map/vmap()/while/body/eval_jaxpr/scatter-add | solution.py:64
  323.8 7.0 %fusion.110 = f32[8,512,64]{2,1,0:T(8,128)} fusion(f32[8,64,512]{2,1,0:T(8,128)} %fusion.106, bf16[6,1,8,64,64]{4,3,2,1,0:T(8,128)(2,1)} %get-tuple-element.266, s32[]{:T(128)} %get-tuple-element.247, f32[8,64,512]{2,1,0:T(8,128)} %get-tuple-element.233, f32[8,64]{1,0:T(8,128)S(1)} %get-tuple-element.234), kind=kOutput, calls=%fused_computation.26.clone.1 | convolution fusion | flops 35390464 | bytes 5382656 | tf_op jit(solution)/shard_map/vmap()/while/body/eval_jaxpr/reshape | solution.py:62
  330.8 7.0 %scatter_fusion = f32[48,64,64]{2,1,0:T(8,128)S(1)} fusion(f32[48,64,64]{2,1,0:T(8,128)S(1)} %bitcast.153, s32[64]{0:T(128)S(1)} %reshape.343, f32[64,64,64]{2,1,0:T(8,128)} %bitcast.162), kind=kCustom, calls=%fused_computation.6.clone.1 | custom fusion | flops 262144 | bytes 3145984 | tf_op jit(solution)/shard_map/vmap()/while/body/eval_jaxpr/scatter-add | solution.py:61
  354.2 6.0 fusion.113
  364.4 7.0 %scatter_fusion.1 = f32[48,64,64]{2,1,0:T(8,128)S(1)} fusion(f32[48,64,64]{2,1,0:T(8,128)S(1)} %bitcast.155, s32[64]{0:T(128)S(1)} %reshape.343, f32[64,64,64]{2,1,0:T(8,128)} %bitcast.163), kind=kCustom, calls=%fused_computation.7.clone.1 | custom fusion | flops 262144 | bytes 3145984 | tf_op jit(solution)/shard_map/vmap()/while/body/eval_jaxpr/scatter-add | solution.py:64
  371.5 7.0 %fusion.110 = f32[8,512,64]{2,1,0:T(8,128)} fusion(f32[8,64,512]{2,1,0:T(8,128)} %fusion.106, bf16[6,1,8,64,64]{4,3,2,1,0:T(8,128)(2,1)} %get-tuple-element.266, s32[]{:T(128)} %get-tuple-element.247, f32[8,64,512]{2,1,0:T(8,128)} %get-tuple-element.233, f32[8,64]{1,0:T(8,128)S(1)} %get-tuple-element.234), kind=kOutput, calls=%fused_computation.26.clone.1 | convolution fusion | flops 35390464 | bytes 5382656 | tf_op jit(solution)/shard_map/vmap()/while/body/eval_jaxpr/reshape | solution.py:62
  378.5 7.0 %scatter_fusion = f32[48,64,64]{2,1,0:T(8,128)S(1)} fusion(f32[48,64,64]{2,1,0:T(8,128)S(1)} %bitcast.153, s32[64]{0:T(128)S(1)} %reshape.343, f32[64,64,64]{2,1,0:T(8,128)} %bitcast.162), kind=kCustom, calls=%fused_computation.6.clone.1 | custom fusion | flops 262144 | bytes 3145984 | tf_op jit(solution)/shard_map/vmap()/while/body/eval_jaxpr/scatter-add | solution.py:61
  412.2 7.0 %scatter_fusion.1 = f32[48,64,64]{2,1,0:T(8,128)S(1)} fusion(f32[48,64,64]{2,1,0:T(8,128)S(1)} %bitcast.155, s32[64]{0:T(128)S(1)} %reshape.343, f32[64,64,64]{2,1,0:T(8,128)} %bitcast.163), kind=kCustom, calls=%fused_computation.7.clone.1 | custom fusion | flops 262144 | bytes 3145984 | tf_op jit(solution)/shard_map/vmap()/while/body/eval_jaxpr/scatter-add | solution.py:64
  419.2 7.0 %fusion.110 = f32[8,512,64]{2,1,0:T(8,128)} fusion(f32[8,64,512]{2,1,0:T(8,128)} %fusion.106, bf16[6,1,8,64,64]{4,3,2,1,0:T(8,128)(2,1)} %get-tuple-element.266, s32[]{:T(128)} %get-tuple-element.247, f32[8,64,512]{2,1,0:T(8,128)} %get-tuple-element.233, f32[8,64]{1,0:T(8,128)S(1)} %get-tuple-element.234), kind=kOutput, calls=%fused_computation.26.clone.1 | convolution fusion | flops 35390464 | bytes 5382656 | tf_op jit(solution)/shard_map/vmap()/while/body/eval_jaxpr/reshape | solution.py:62
  426.2 7.0 %scatter_fusion = f32[48,64,64]{2,1,0:T(8,128)S(1)} fusion(f32[48,64,64]{2,1,0:T(8,128)S(1)} %bitcast.153, s32[64]{0:T(128)S(1)} %reshape.343, f32[64,64,64]{2,1,0:T(8,128)} %bitcast.162), kind=kCustom, calls=%fused_computation.6.clone.1 | custom fusion | flops 262144 | bytes 3145984 | tf_op jit(solution)/shard_map/vmap()/while/body/eval_jaxpr/scatter-add | solution.py:61
  438.9 9.2 %gather_fusion.4 = bf16[3072,64]{1,0:T(8,128)(2,1)S(1)} fusion(bf16[3072,64]{1,0:T(8,128)(2,1)S(1)} %bitcast.164, s32[3072]{0:T(1024)S(1)} %fusion.52), kind=kCustom, calls=%fused_computation.4 | custom fusion | bytes 798720 | tf_op jit(solution)/shard_map/gather | solution.py:118
  459.1 11.1 %gather_fusion.5 = bf16[3072,192]{1,0:T(8,128)(2,1)S(1)} fusion(bf16[3072,192]{1,0:T(8,128)(2,1)S(1)} %maximum_bitcast_fusion, s32[3072]{0:T(1024)S(1)} %fusion.52), kind=kCustom, calls=%fused_computation.5 | custom fusion | bytes 2371584 | tf_op jit(solution)/shard_map/gather | solution.py:117
  474.5 7.3 %all-to-all-start.3 = ((bf16[16,2,18432]{2,1,0:T(2,128)(2,1)}), bf16[16,2,18432]{2,1,0:T(2,128)(2,1)}, u32[]{:S(2)}, u32[]{:S(2)}) async-start(bf16[16,2,18432]{2,1,0:T(2,128)(2,1)} %reshape.324), calls=%async_computation.3 | async-start | bytes 2359296 | tf_op jit(solution)/shard_map/all_to_all | solution.py:121
  491.1 101.6 %reduce-scatter.4.cloned.1.call-done = bf16[32,192]{1,0:T(8,128)(2,1)} async-done(((bf16[1024,192]{1,0:T(8,128)(2,1)}), bf16[32,192]{1,0:T(8,128)(2,1)}) %reduce-scatter.4.cloned.1.call-update) | async-done | bytes 12304
  594.2 8.4 %reshape.325 = bf16[3072,1,192]{2,1,0:T(2,128)(2,1)S(1)} reshape(bf16[16,2,18432]{2,1,0:T(2,128)(2,1)} %all-to-all-done.3) | data formatting | bytes 2359296
  602.6 6.2 copy.102
  (164 shorter events, 216.7 us)
Async XLA Ops:
  7.2 84.3 %copy-start.3 = (bf16[1,192,1024]{2,1,0:T(8,128)(2,1)S(1)}, bf16[1,192,1024]{2,1,0:T(8,128)(2,1)}, u32[]{:S(2)}) copy-start(bf16[1,192,1024]{2,1,0:T(8,128)(2,1)} %param.8) | copy-start | bytes 1179652
  7.2 12.7 %copy-start.5 = (s32[1,48,8]{1,2,0:T(8,128)S(1)}, s32[1,48,8]{1,2,0:T(8,128)}, u32[]{:S(2)}) copy-start(s32[1,48,8]{1,2,0:T(8,128)} %param.12) | copy-start | bytes 4612
  7.2 13.3 %copy-start.6 = (s32[1,48]{1,0:T(1,128)S(1)}, s32[1,48]{1,0:T(1,128)}, u32[]{:S(2)}) copy-start(s32[1,48]{1,0:T(1,128)} %param.13) | copy-start | bytes 580
  7.2 84.3 %all-gather.4.cloned.1.call-start = ((), (), s32[]{:S(2)}) async-start(), calls=%async_computation.5 | async-start | bytes 6488064 | tf_op jit(solution)/shard_map/all_gather | solution.py:88
  9.9 91.6 %all-to-all-start.1 = ((bf16[192,16,64]{0,2,1:T(8,128)(2,1)}), bf16[192,16,64]{0,2,1:T(8,128)(2,1)S(1)}, u32[]{:S(2)}, u32[]{:S(2)}) async-start(bf16[192,16,64]{0,2,1:T(8,128)(2,1)} %bitcast.27), calls=%async_computation.1 | async-start | bytes 1048576 | tf_op jit(solution)/shard_map/all_to_all | solution.py:97
  19.1 462.7 %all-gather.6.cloned.1.call-start = ((), (), s32[]{:S(2)}) async-start(), calls=%async_computation.6 | async-start | bytes 6684672 | tf_op jit(solution)/shard_map/all_gather | solution.py:89
  101.5 7.4 %copy-start.4 = (s32[1,3072]{1,0:T(1,128)S(1)}, s32[1,3072]{1,0:T(1,128)}, u32[]{:S(2)}) copy-start(s32[1,3072]{1,0:T(1,128)} %param.11) | copy-start | bytes 36868
  101.5 35.7 %all-to-all-start = ((bf16[192,16,192]{2,0,1:T(8,128)(2,1)}), bf16[192,16,192]{2,0,1:T(8,128)(2,1)S(1)}, u32[]{:S(2)}, u32[]{:S(2)}) async-start(bf16[192,16,192]{2,0,1:T(8,128)(2,1)} %copy.93), calls=%async_computation | async-start | bytes 3145728 | tf_op jit(solution)/shard_map/all_to_all | solution.py:96
  155.4 1.0 copy-start
  203.2 1.0 copy-start
  250.9 1.0 copy-start
  298.6 1.0 copy-start
  346.3 1.0 copy-start
  394.0 1.0 copy-start
  437.8 1.1 copy-start.1
  448.6 8.6 %copy-start.2 = (bf16[1,48,64,64]{3,2,1,0:T(8,128)(2,1)S(1)}, bf16[1,48,64,64]{3,2,1,0:T(8,128)(2,1)}, u32[]{:S(2)}) copy-start(bf16[1,48,64,64]{3,2,1,0:T(8,128)(2,1)} %convert_element_type.62) | copy-start | bytes 1179652
  451.4 23.1 %all-to-all-start.2 = ((bf16[16,2,6144]{2,1,0:T(2,128)(2,1)}), bf16[16,2,6144]{2,1,0:T(2,128)(2,1)S(1)}, u32[]{:S(2)}, u32[]{:S(2)}) async-start(bf16[16,2,6144]{2,1,0:T(2,128)(2,1)} %reshape.322), calls=%async_computation.2 | async-start | bytes 786432 | tf_op jit(solution)/shard_map/all_to_all | solution.py:120
  474.5 119.7 %all-to-all-start.3 = ((bf16[16,2,18432]{2,1,0:T(2,128)(2,1)}), bf16[16,2,18432]{2,1,0:T(2,128)(2,1)}, u32[]{:S(2)}, u32[]{:S(2)}) async-start(bf16[16,2,18432]{2,1,0:T(2,128)(2,1)} %reshape.324), calls=%async_computation.3 | async-start | bytes 2359296 | tf_op jit(solution)/shard_map/all_to_all | solution.py:121
  481.7 110.9 %reduce-scatter.4.cloned.1.call-start = ((), (), s32[]{:S(2)}) async-start(), calls=%async_computation.7 | async-start | bytes 540672
Sparse Core Ops, SparseCore 0:
  10.2 81.2 all-gather.3
  94.5 83.8 all-gather.5
  487.2 105.4 reduce-scatter.3
where the time goes:
time: 633 us; the launch traced here: 628 us
  waiting for transfers between devices  178 us (28%)
  matrix products  168 us (27%)
  local copies, waits for them, and re-layouts  140 us (22%)
  other arithmetic  99 us (16%)
  starting transfers between devices  29.8 us (5%)
  between operations  14 us (2%)
    unnamed x4, waiting for transfers between devices  103 us
    all_gather x1, waiting for transfers between devices, per_device(): weights_all = lax.all_gather(qkv_weight, 'dp', axis=0, tiled=True)  70.2 us
    reshape x6, matrix products, group_step(): key_terms.reshape(in_group, slot_count, block_rows, head_width)  42.2 us
    scatter-add x6, other arithmetic, group_step(): grad_value.at[block_ids]  42 us
    scatter-add x6, other arithmetic, group_step(): grad_key.at[block_ids]  42 us
    dot_general x6, matrix products, group_step(): jnp.einsum('cqk,cke->cqe', grad_scores, key_rows, preferred_element_type=...  36 us
    reshape x6, matrix products, group_step(): value_terms.reshape(in_group, slot_count, block_rows, head_width)  25.7 us
    dot_general x6, matrix products, group_step(): jnp.einsum('cqk,cke->cqe', attn_low, value_rows, preferred_element_type=j...  21 us
  transfers between devices with their start and end apart: 7, of which 3 were waited for; matrix products, arithmetic and copies ran while one was open for 59% of the time, Pallas kernels for 0%

commit v1 on v0

--- a/solution.py
+++ b/solution.py
@@ -6,6 +6,22 @@
 
 HEADS = 16
 HD = 64
+
+
+def exchange_in_pairs(value, axis, split, join):
+    ways, here = (lax.axis_size(axis), lax.axis_index(axis))
+    width = value.shape[split] // ways
+    dims = list(value.shape)
+    dims[split] = width
+    height = dims[join]
+    dims[join] = height * ways
+    full = jnp.zeros(dims, value.dtype)
+    for mask in range(ways):
+        part = lax.dynamic_slice_in_dim(value, (here ^ mask) * width, width, axis=split)
+        if mask:
+            part = lax.ppermute(part, axis, [(d, d ^ mask) for d in range(ways)])
+        full = lax.dynamic_update_slice_in_dim(full, part, (here ^ mask) * height, axis=join)
+    return full
 
 
 def attend(query, key_in, value, grad_out, blocks, counts):
@@ -118,7 +134,7 @@
     output_nodes = output_all[inverse]
     output_back, grad_back = (
         lax.all_to_all(output_nodes, "seq", split_axis=0, concat_axis=1, tiled=True),
-        lax.all_to_all(grad_heads, "seq", split_axis=0, concat_axis=1, tiled=True),
+        exchange_in_pairs(grad_heads, "seq", 0, 1),
     )
     attended = output_back.reshape(1, local_rows, model_width)
     grad_local = grad_back.reshape(local_rows, 3 * model_width)

time: 633 us -> 607 us (0.959)
  the two profiles are of different devices: /device:TPU:8 before, /device:TPU:34 now
where the time goes in v1:
time: 607 us; the launch traced here: 602 us
  local copies, waits for them, and re-layouts  167 us (28%)
  matrix products  166 us (27%)
  other arithmetic  95.1 us (16%)
  starting transfers between devices  81.9 us (13%)
  waiting for transfers between devices  77.1 us (13%)
  between operations  14.8 us (2%)
    all_gather x1, waiting for transfers between devices, per_device(): weights_all = lax.all_gather(qkv_weight, 'dp', axis=0, tiled=True)  71.8 us
    ppermute x15, starting transfers between devices, exchange_in_pairs(): part = lax.ppermute(part, axis, [(d, d ^ mask) for d in range(ways)])  58.3 us
    dynamic_update_slice x16, local copies, waits for them, and re-layouts, exchange_in_pairs(): lax.dynamic_update_slice_in_dim(full, part, (here ^ mask) * height, axis=...  43.4 us
    scatter-add x6, other arithmetic, group_step(): grad_value.at[block_ids]  42 us
    scatter-add x6, other arithmetic, group_step(): grad_key.at[block_ids]  42 us
    reshape x6, matrix products, group_step(): key_terms.reshape(in_group, slot_count, block_rows, head_width)  41.5 us
    dot_general x6, matrix products, group_step(): jnp.einsum('cqk,cke->cqe', grad_scores, key_rows, preferred_element_type=...  35.5 us
    reshape x6, matrix products, group_step(): value_terms.reshape(in_group, slot_count, block_rows, head_width)  25.6 us
  transfers between devices with their start and end apart: 21, of which 2 were waited for; matrix products, arithmetic and copies ran while one was open for 69% of the time, Pallas kernels for 0%

profile of v1, /device:TPU:34, one launch (start us, length us, event | category | flops | bytes accessed | tf_op | source)
XLA Modules:
  0.0 602.5 jit_solution(15964244420693973315)
XLA Ops:
  9.9 7.5 %all-to-all-start.1 = ((bf16[192,16,64]{0,2,1:T(8,128)(2,1)}), bf16[192,16,64]{0,2,1:T(8,128)(2,1)S(1)}, u32[]{:S(2)}, u32[]{:S(2)}) async-start(bf16[192,16,64]{0,2,1:T(8,128)(2,1)} %bitcast.27), calls=%async_computation.1 | async-start | bytes 1048576 | tf_op jit(solution)/shard_map/all_to_all | solution.py:113
  19.6 71.8 %all-gather.4.cloned.1.call-done = bf16[1024,3072]{1,0:T(8,128)(2,1)} async-done(((bf16[32,3072]{1,0:T(8,128)(2,1)}), bf16[1024,3072]{1,0:T(8,128)(2,1)}) %all-gather.4.cloned.1.call-update) | async-done | bytes 6291472 | tf_op jit(solution)/shard_map/all_gather | solution.py:104
  101.4 7.4 %all-to-all-start = ((bf16[192,16,192]{2,0,1:T(8,128)(2,1)}), bf16[192,16,192]{2,0,1:T(8,128)(2,1)S(1)}, u32[]{:S(2)}, u32[]{:S(2)}) async-start(bf16[192,16,192]{2,0,1:T(8,128)(2,1)} %copy.121), calls=%async_computation | async-start | bytes 3145728 | tf_op jit(solution)/shard_map/all_to_all | solution.py:112
  108.9 12.0 %scatter_custom_fusion.2 = s32[3072]{0:T(1024)S(1)} fusion(s32[3072]{0:T(1024)S(1)} %bitcast.204, s32[3072]{0:T(1024)S(1)} %iota.7, s32[]{:T(128)} %constant.7.clone.1), kind=kCustom, calls=%fused_computation.87 | custom fusion | bytes 12292 | tf_op jit(solution)/shard_map/scatter | solution.py:119
  121.3 11.4 %gather_fusion.3 = bf16[3072,64]{1,0:T(8,128)(2,1)} fusion(bf16[3072,64]{1,0:T(8,128)(2,1)S(1)} %bitcast.185, s32[3072]{0:T(1024)S(1)} %broadcast_clamp_fusion), kind=kCustom, calls=%fused_computation.3 | custom fusion | bytes 798720 | tf_op jit(solution)/shard_map/gather | solution.py:122
  136.5 11.1 %gather_fusion.2 = bf16[3072,192]{1,0:T(8,128)(2,1)S(1)} fusion(bf16[3072,192]{1,0:T(8,128)(2,1)S(1)} %bitcast.176, s32[3072]{0:T(1024)S(1)} %broadcast_clamp_fusion), kind=kCustom, calls=%fused_computation.2 | custom fusion | bytes 2371584 | tf_op jit(solution)/shard_map/gather | solution.py:121
  149.8 284.6 %while.16 = (s32[]{:T(128)}, f32[1,48,64,64]{3,2,1,0:T(8,128)S(1)}, f32[1,48,64,64]{3,2,1,0:T(8,128)S(1)}, bf16[6,1,8,64,64]{4,3,2,1,0:T(8,128)(2,1)}, bf16[6,1,...) while((s32[]{:T(128)}, f32[1,48,64,64]{3,2,1,0:T(8,128)S(1)}, ...), condition=%wide.region_6.7_spmd, body=%wide.region_0.6_spmd.sunk | while | flops 209000192 | bytes 36499064 | solution.py:86
  172.8 7.0 %scatter_fusion.1 = f32[48,64,64]{2,1,0:T(8,128)S(1)} fusion(f32[48,64,64]{2,1,0:T(8,128)S(1)} %bitcast.179, s32[64]{0:T(128)S(1)} %reshape.356, f32[64,64,64]{2,1,0:T(8,128)} %bitcast.187), kind=kCustom, calls=%fused_computation.7.clone.1 | custom fusion | flops 262144 | bytes 3145984 | tf_op jit(solution)/shard_map/vmap()/while/body/eval_jaxpr/scatter-add | solution.py:80
  179.8 6.9 %fusion.110 = f32[8,512,64]{2,1,0:T(8,128)} fusion(f32[8,64,512]{2,1,0:T(8,128)} %fusion.106, bf16[6,1,8,64,64]{4,3,2,1,0:T(8,128)(2,1)} %get-tuple-element.282, s32[]{:T(128)} %get-tuple-element.263, f32[8,64,512]{2,1,0:T(8,128)} %get-tuple-element.249, f32[8,64]{1,0:T(8,128)S(1)} %get-tuple-element.250), kind=kOutput, calls=%fused_computation.26.clone.1 | convolution fusion | flops 35390464 | bytes 5382656 | tf_op jit(solution)/shard_map/vmap()/while/body/eval_jaxpr/reshape | solution.py:78
  186.8 7.0 %scatter_fusion = f32[48,64,64]{2,1,0:T(8,128)S(1)} fusion(f32[48,64,64]{2,1,0:T(8,128)S(1)} %bitcast.177, s32[64]{0:T(128)S(1)} %reshape.356, f32[64,64,64]{2,1,0:T(8,128)} %bitcast.186), kind=kCustom, calls=%fused_computation.6.clone.1 | custom fusion | flops 262144 | bytes 3145984 | tf_op jit(solution)/shard_map/vmap()/while/body/eval_jaxpr/scatter-add | solution.py:77
  220.3 7.0 %scatter_fusion.1 = f32[48,64,64]{2,1,0:T(8,128)S(1)} fusion(f32[48,64,64]{2,1,0:T(8,128)S(1)} %bitcast.179, s32[64]{0:T(128)S(1)} %reshape.356, f32[64,64,64]{2,1,0:T(8,128)} %bitcast.187), kind=kCustom, calls=%fused_computation.7.clone.1 | custom fusion | flops 262144 | bytes 3145984 | tf_op jit(solution)/shard_map/vmap()/while/body/eval_jaxpr/scatter-add | solution.py:80
  227.3 6.9 %fusion.110 = f32[8,512,64]{2,1,0:T(8,128)} fusion(f32[8,64,512]{2,1,0:T(8,128)} %fusion.106, bf16[6,1,8,64,64]{4,3,2,1,0:T(8,128)(2,1)} %get-tuple-element.282, s32[]{:T(128)} %get-tuple-element.263, f32[8,64,512]{2,1,0:T(8,128)} %get-tuple-element.249, f32[8,64]{1,0:T(8,128)S(1)} %get-tuple-element.250), kind=kOutput, calls=%fused_computation.26.clone.1 | convolution fusion | flops 35390464 | bytes 5382656 | tf_op jit(solution)/shard_map/vmap()/while/body/eval_jaxpr/reshape | solution.py:78
  234.2 7.0 %scatter_fusion = f32[48,64,64]{2,1,0:T(8,128)S(1)} fusion(f32[48,64,64]{2,1,0:T(8,128)S(1)} %bitcast.177, s32[64]{0:T(128)S(1)} %reshape.356, f32[64,64,64]{2,1,0:T(8,128)} %bitcast.186), kind=kCustom, calls=%fused_computation.6.clone.1 | custom fusion | flops 262144 | bytes 3145984 | tf_op jit(solution)/shard_map/vmap()/while/body/eval_jaxpr/scatter-add | solution.py:77
  267.7 7.0 %scatter_fusion.1 = f32[48,64,64]{2,1,0:T(8,128)S(1)} fusion(f32[48,64,64]{2,1,0:T(8,128)S(1)} %bitcast.179, s32[64]{0:T(128)S(1)} %reshape.356, f32[64,64,64]{2,1,0:T(8,128)} %bitcast.187), kind=kCustom, calls=%fused_computation.7.clone.1 | custom fusion | flops 262144 | bytes 3145984 | tf_op jit(solution)/shard_map/vmap()/while/body/eval_jaxpr/scatter-add | solution.py:80
  274.7 6.9 %fusion.110 = f32[8,512,64]{2,1,0:T(8,128)} fusion(f32[8,64,512]{2,1,0:T(8,128)} %fusion.106, bf16[6,1,8,64,64]{4,3,2,1,0:T(8,128)(2,1)} %get-tuple-element.282, s32[]{:T(128)} %get-tuple-element.263, f32[8,64,512]{2,1,0:T(8,128)} %get-tuple-element.249, f32[8,64]{1,0:T(8,128)S(1)} %get-tuple-element.250), kind=kOutput, calls=%fused_computation.26.clone.1 | convolution fusion | flops 35390464 | bytes 5382656 | tf_op jit(solution)/shard_map/vmap()/while/body/eval_jaxpr/reshape | solution.py:78
  281.6 7.0 %scatter_fusion = f32[48,64,64]{2,1,0:T(8,128)S(1)} fusion(f32[48,64,64]{2,1,0:T(8,128)S(1)} %bitcast.177, s32[64]{0:T(128)S(1)} %reshape.356, f32[64,64,64]{2,1,0:T(8,128)} %bitcast.186), kind=kCustom, calls=%fused_computation.6.clone.1 | custom fusion | flops 262144 | bytes 3145984 | tf_op jit(solution)/shard_map/vmap()/while/body/eval_jaxpr/scatter-add | solution.py:77
  315.1 7.0 %scatter_fusion.1 = f32[48,64,64]{2,1,0:T(8,128)S(1)} fusion(f32[48,64,64]{2,1,0:T(8,128)S(1)} %bitcast.179, s32[64]{0:T(128)S(1)} %reshape.356, f32[64,64,64]{2,1,0:T(8,128)} %bitcast.187), kind=kCustom, calls=%fused_computation.7.clone.1 | custom fusion | flops 262144 | bytes 3145984 | tf_op jit(solution)/shard_map/vmap()/while/body/eval_jaxpr/scatter-add | solution.py:80
  322.1 6.9 %fusion.110 = f32[8,512,64]{2,1,0:T(8,128)} fusion(f32[8,64,512]{2,1,0:T(8,128)} %fusion.106, bf16[6,1,8,64,64]{4,3,2,1,0:T(8,128)(2,1)} %get-tuple-element.282, s32[]{:T(128)} %get-tuple-element.263, f32[8,64,512]{2,1,0:T(8,128)} %get-tuple-element.249, f32[8,64]{1,0:T(8,128)S(1)} %get-tuple-element.250), kind=kOutput, calls=%fused_computation.26.clone.1 | convolution fusion | flops 35390464 | bytes 5382656 | tf_op jit(solution)/shard_map/vmap()/while/body/eval_jaxpr/reshape | solution.py:78
  329.1 7.0 %scatter_fusion = f32[48,64,64]{2,1,0:T(8,128)S(1)} fusion(f32[48,64,64]{2,1,0:T(8,128)S(1)} %bitcast.177, s32[64]{0:T(128)S(1)} %reshape.356, f32[64,64,64]{2,1,0:T(8,128)} %bitcast.186), kind=kCustom, calls=%fused_computation.6.clone.1 | custom fusion | flops 262144 | bytes 3145984 | tf_op jit(solution)/shard_map/vmap()/while/body/eval_jaxpr/scatter-add | solution.py:77
  362.5 7.0 %scatter_fusion.1 = f32[48,64,64]{2,1,0:T(8,128)S(1)} fusion(f32[48,64,64]{2,1,0:T(8,128)S(1)} %bitcast.179, s32[64]{0:T(128)S(1)} %reshape.356, f32[64,64,64]{2,1,0:T(8,128)} %bitcast.187), kind=kCustom, calls=%fused_computation.7.clone.1 | custom fusion | flops 262144 | bytes 3145984 | tf_op jit(solution)/shard_map/vmap()/while/body/eval_jaxpr/scatter-add | solution.py:80
  369.5 6.9 %fusion.110 = f32[8,512,64]{2,1,0:T(8,128)} fusion(f32[8,64,512]{2,1,0:T(8,128)} %fusion.106, bf16[6,1,8,64,64]{4,3,2,1,0:T(8,128)(2,1)} %get-tuple-element.282, s32[]{:T(128)} %get-tuple-element.263, f32[8,64,512]{2,1,0:T(8,128)} %get-tuple-element.249, f32[8,64]{1,0:T(8,128)S(1)} %get-tuple-element.250), kind=kOutput, calls=%fused_computation.26.clone.1 | convolution fusion | flops 35390464 | bytes 5382656 | tf_op jit(solution)/shard_map/vmap()/while/body/eval_jaxpr/reshape | solution.py:78
  376.5 7.0 %scatter_fusion = f32[48,64,64]{2,1,0:T(8,128)S(1)} fusion(f32[48,64,64]{2,1,0:T(8,128)S(1)} %bitcast.177, s32[64]{0:T(128)S(1)} %reshape.356, f32[64,64,64]{2,1,0:T(8,128)} %bitcast.186), kind=kCustom, calls=%fused_computation.6.clone.1 | custom fusion | flops 262144 | bytes 3145984 | tf_op jit(solution)/shard_map/vmap()/while/body/eval_jaxpr/scatter-add | solution.py:77
  399.8 5.9 fusion.113
  410.0 7.0 %scatter_fusion.1 = f32[48,64,64]{2,1,0:T(8,128)S(1)} fusion(f32[48,64,64]{2,1,0:T(8,128)S(1)} %bitcast.179, s32[64]{0:T(128)S(1)} %reshape.356, f32[64,64,64]{2,1,0:T(8,128)} %bitcast.187), kind=kCustom, calls=%fused_computation.7.clone.1 | custom fusion | flops 262144 | bytes 3145984 | tf_op jit(solution)/shard_map/vmap()/while/body/eval_jaxpr/scatter-add | solution.py:80
  417.0 6.9 %fusion.110 = f32[8,512,64]{2,1,0:T(8,128)} fusion(f32[8,64,512]{2,1,0:T(8,128)} %fusion.106, bf16[6,1,8,64,64]{4,3,2,1,0:T(8,128)(2,1)} %get-tuple-element.282, s32[]{:T(128)} %get-tuple-element.263, f32[8,64,512]{2,1,0:T(8,128)} %get-tuple-element.249, f32[8,64]{1,0:T(8,128)S(1)} %get-tuple-element.250), kind=kOutput, calls=%fused_computation.26.clone.1 | convolution fusion | flops 35390464 | bytes 5382656 | tf_op jit(solution)/shard_map/vmap()/while/body/eval_jaxpr/reshape | solution.py:78
  423.9 7.0 %scatter_fusion = f32[48,64,64]{2,1,0:T(8,128)S(1)} fusion(f32[48,64,64]{2,1,0:T(8,128)S(1)} %bitcast.177, s32[64]{0:T(128)S(1)} %reshape.356, f32[64,64,64]{2,1,0:T(8,128)} %bitcast.186), kind=kCustom, calls=%fused_computation.6.clone.1 | custom fusion | flops 262144 | bytes 3145984 | tf_op jit(solution)/shard_map/vmap()/while/body/eval_jaxpr/scatter-add | solution.py:77
  436.5 11.1 %gather_fusion.5 = bf16[3072,192]{1,0:T(8,128)(2,1)S(1)} fusion(bf16[3072,192]{1,0:T(8,128)(2,1)S(1)} %maximum_bitcast_fusion, s32[3072]{0:T(1024)S(1)} %fusion.52), kind=kCustom, calls=%fused_computation.5 | custom fusion | bytes 2371584 | tf_op jit(solution)/shard_map/gather | solution.py:133
  466.5 6.6 %collective-permute-start.4 = (bf16[192,1,192]{2,0,1:T(8,128)(2,1)S(1)}, bf16[192,1,192]{2,0,1:T(8,128)(2,1)S(1)}, u32[]{:S(2)}, u32[]{:S(2)}) collective-permute-start(bf16[192,1,192]{2,0,1:T(8,128)(2,1)S(1)} %get-tuple-element.171), channel_id=1, source_target_pairs={{0,5},{1,4},{2,7},{3,6},{4,1},{5,0},{6,3},{7,2},{8,13},{9,12},{10,... | collective-permute-start | bytes 221192 | tf_op jit(solution)/shard_map/ppermute | solution.py:22
  481.9 7.4 %collective-permute-start.8 = (bf16[192,1,192]{2,0,1:T(8,128)(2,1)S(1)}, bf16[192,1,192]{2,0,1:T(8,128)(2,1)S(1)}, u32[]{:S(2)}, u32[]{:S(2)}) collective-permute-start(bf16[192,1,192]{2,0,1:T(8,128)(2,1)S(1)} %get-tuple-element.167), channel_id=1, source_target_pairs={{0,9},{1,8},{2,11},{3,10},{4,13},{5,12},{6,15},{7,14},{8,1},{9,0},... | collective-permute-start | bytes 221192 | tf_op jit(solution)/shard_map/ppermute | solution.py:22
  498.7 8.1 %collective-permute-start.12 = (bf16[192,1,192]{2,0,1:T(8,128)(2,1)S(1)}, bf16[192,1,192]{2,0,1:T(8,128)(2,1)S(1)}, u32[]{:S(2)}, u32[]{:S(2)}) collective-permute-start(bf16[192,1,192]{2,0,1:T(8,128)(2,1)S(1)} %get-tuple-element.163), channel_id=1, source_target_pairs={{0,13},{1,12},{2,15},{3,14},{4,9},{5,8},{6,11},{7,10},{8,5},{9,4},... | collective-permute-start | bytes 221192 | tf_op jit(solution)/shard_map/ppermute | solution.py:22
  513.2 9.2 %gather_fusion.4 = bf16[3072,64]{1,0:T(8,128)(2,1)S(1)} fusion(bf16[3072,64]{1,0:T(8,128)(2,1)S(1)} %bitcast.188, s32[3072]{0:T(1024)S(1)} %fusion.52), kind=kCustom, calls=%fused_computation.4 | custom fusion | bytes 798720 | tf_op jit(solution)/shard_map/gather | solution.py:134
  525.6 8.6 %all-to-all-start.2 = ((bf16[16,2,6144]{2,1,0:T(2,128)(2,1)}), bf16[16,2,6144]{2,1,0:T(2,128)(2,1)S(1)}, u32[]{:S(2)}, u32[]{:S(2)}) async-start(bf16[16,2,6144]{2,1,0:T(2,128)(2,1)} %reshape.337), calls=%async_computation.2 | async-start | bytes 786432 | tf_op jit(solution)/shard_map/all_to_all | solution.py:136
  (230 shorter events, 283.9 us)
Async XLA Ops:
  7.2 84.3 %copy-start.3 = (bf16[1,192,1024]{2,1,0:T(8,128)(2,1)S(1)}, bf16[1,192,1024]{2,1,0:T(8,128)(2,1)}, u32[]{:S(2)}) copy-start(bf16[1,192,1024]{2,1,0:T(8,128)(2,1)} %param.8) | copy-start | bytes 1179652
  7.2 11.1 %copy-start.10 = (s32[1,48,8]{1,2,0:T(8,128)S(1)}, s32[1,48,8]{1,2,0:T(8,128)}, u32[]{:S(2)}) copy-start(s32[1,48,8]{1,2,0:T(8,128)} %param.12) | copy-start | bytes 4612
  7.2 11.7 %copy-start.11 = (s32[1,48]{1,0:T(1,128)S(1)}, s32[1,48]{1,0:T(1,128)}, u32[]{:S(2)}) copy-start(s32[1,48]{1,0:T(1,128)} %param.13) | copy-start | bytes 580
  7.2 84.3 %all-gather.4.cloned.1.call-start = ((), (), s32[]{:S(2)}) async-start(), calls=%async_computation.4 | async-start | bytes 6488064 | tf_op jit(solution)/shard_map/all_gather | solution.py:104
  9.9 91.5 %all-to-all-start.1 = ((bf16[192,16,64]{0,2,1:T(8,128)(2,1)}), bf16[192,16,64]{0,2,1:T(8,128)(2,1)S(1)}, u32[]{:S(2)}, u32[]{:S(2)}) async-start(bf16[192,16,64]{0,2,1:T(8,128)(2,1)} %bitcast.27), calls=%async_computation.1 | async-start | bytes 1048576 | tf_op jit(solution)/shard_map/all_to_all | solution.py:113
  17.4 430.2 %all-gather.6.cloned.1.call-start = ((), (), s32[]{:S(2)}) async-start(), calls=%async_computation.5 | async-start | bytes 6684672 | tf_op jit(solution)/shard_map/all_gather | solution.py:105
  101.4 7.5 %copy-start.9 = (s32[1,3072]{1,0:T(1,128)S(1)}, s32[1,3072]{1,0:T(1,128)}, u32[]{:S(2)}) copy-start(s32[1,3072]{1,0:T(1,128)} %param.11) | copy-start | bytes 36868
  101.4 35.1 %all-to-all-start = ((bf16[192,16,192]{2,0,1:T(8,128)(2,1)}), bf16[192,16,192]{2,0,1:T(8,128)(2,1)S(1)}, u32[]{:S(2)}, u32[]{:S(2)}) async-start(bf16[192,16,192]{2,0,1:T(8,128)(2,1)} %copy.121), calls=%async_computation | async-start | bytes 3145728 | tf_op jit(solution)/shard_map/all_to_all | solution.py:112
  108.8 485.6 %reduce-scatter.4.cloned.1.call-start = ((), (), s32[]{:S(2)}) async-start(), calls=%async_computation.6 | async-start | bytes 540672
  249.7 1.0 copy-start
  434.6 1.1 copy-start.2
  452.8 60.3 %copy-start.1 = (bf16[6,1,8,64,64]{4,3,2,1,0:T(8,128)(2,1)S(1)}, bf16[6,1,8,64,64]{4,3,2,1,0:T(8,128)(2,1)}, u32[]{:S(2)}) copy-start(bf16[6,1,8,64,64]{4,3,2,1,0:T(8,128)(2,1)} %get-tuple-element.63) | copy-start | bytes 1179652
  453.7 19.4 %collective-permute-start = (bf16[192,1,192]{2,0,1:T(8,128)(2,1)S(1)}, bf16[192,1,192]{2,0,1:T(8,128)(2,1)S(1)}, u32[]{:S(2)}, u32[]{:S(2)}) collective-permute-start(bf16[192,1,192]{2,0,1:T(8,128)(2,1)S(1)} %get-tuple-element.175), channel_id=1, source_target_pairs={{0,1},{1,0},{2,3},{3,2},{4,5},{5,4},{6,7},{7,6},{8,9},{9,8},{10,11... | collective-permute-start | bytes 221192 | tf_op jit(solution)/shard_map/ppermute | solution.py:22
  459.2 15.8 %collective-permute-start.1 = (bf16[192,1,192]{2,0,1:T(8,128)(2,1)S(1)}, bf16[192,1,192]{2,0,1:T(8,128)(2,1)S(1)}, u32[]{:S(2)}, u32[]{:S(2)}) collective-permute-start(bf16[192,1,192]{2,0,1:T(8,128)(2,1)S(1)} %get-tuple-element.174), channel_id=1, source_target_pairs={{0,2},{1,3},{2,0},{3,1},{4,6},{5,7},{6,4},{7,5},{8,10},{9,11},{10,... | collective-permute-start | bytes 221192 | tf_op jit(solution)/shard_map/ppermute | solution.py:22
  461.2 16.9 %collective-permute-start.2 = (bf16[192,1,192]{2,0,1:T(8,128)(2,1)S(1)}, bf16[192,1,192]{2,0,1:T(8,128)(2,1)S(1)}, u32[]{:S(2)}, u32[]{:S(2)}) collective-permute-start(bf16[192,1,192]{2,0,1:T(8,128)(2,1)S(1)} %get-tuple-element.173), channel_id=1, source_target_pairs={{0,3},{1,2},{2,1},{3,0},{4,7},{5,6},{6,5},{7,4},{8,11},{9,10},{10,... | collective-permute-start | bytes 221192 | tf_op jit(solution)/shard_map/ppermute | solution.py:22
  464.5 17.3 %collective-permute-start.3 = (bf16[192,1,192]{2,0,1:T(8,128)(2,1)S(1)}, bf16[192,1,192]{2,0,1:T(8,128)(2,1)S(1)}, u32[]{:S(2)}, u32[]{:S(2)}) collective-permute-start(bf16[192,1,192]{2,0,1:T(8,128)(2,1)S(1)} %get-tuple-element.172), channel_id=1, source_target_pairs={{0,4},{1,5},{2,6},{3,7},{4,0},{5,1},{6,2},{7,3},{8,12},{9,13},{10,... | collective-permute-start | bytes 221192 | tf_op jit(solution)/shard_map/ppermute | solution.py:22
  466.5 22.9 %collective-permute-start.4 = (bf16[192,1,192]{2,0,1:T(8,128)(2,1)S(1)}, bf16[192,1,192]{2,0,1:T(8,128)(2,1)S(1)}, u32[]{:S(2)}, u32[]{:S(2)}) collective-permute-start(bf16[192,1,192]{2,0,1:T(8,128)(2,1)S(1)} %get-tuple-element.171), channel_id=1, source_target_pairs={{0,5},{1,4},{2,7},{3,6},{4,1},{5,0},{6,3},{7,2},{8,13},{9,12},{10,... | collective-permute-start | bytes 221192 | tf_op jit(solution)/shard_map/ppermute | solution.py:22
  473.1 36.3 %copy-start.4 = (bf16[192,1,192]{2,0,1:T(8,128)(2,1)}, bf16[192,1,192]{2,0,1:T(8,128)(2,1)S(1)}, u32[]{:S(2)}) copy-start(bf16[192,1,192]{2,0,1:T(8,128)(2,1)S(1)} %collective-permute-done) | copy-start | bytes 221188
  473.1 18.2 %collective-permute-start.5 = (bf16[192,1,192]{2,0,1:T(8,128)(2,1)S(1)}, bf16[192,1,192]{2,0,1:T(8,128)(2,1)S(1)}, u32[]{:S(2)}, u32[]{:S(2)}) collective-permute-start(bf16[192,1,192]{2,0,1:T(8,128)(2,1)S(1)} %get-tuple-element.170), channel_id=1, source_target_pairs={{0,6},{1,7},{2,4},{3,5},{4,2},{5,3},{6,0},{7,1},{8,14},{9,15},{10,... | collective-permute-start | bytes 221192 | tf_op jit(solution)/shard_map/ppermute | solution.py:22
  475.0 19.8 %collective-permute-start.6 = (bf16[192,1,192]{2,0,1:T(8,128)(2,1)S(1)}, bf16[192,1,192]{2,0,1:T(8,128)(2,1)S(1)}, u32[]{:S(2)}, u32[]{:S(2)}) collective-permute-start(bf16[192,1,192]{2,0,1:T(8,128)(2,1)S(1)} %get-tuple-element.169), channel_id=1, source_target_pairs={{0,7},{1,6},{2,5},{3,4},{4,3},{5,2},{6,1},{7,0},{8,15},{9,14},{10,... | collective-permute-start | bytes 221192 | tf_op jit(solution)/shard_map/ppermute | solution.py:22
  478.1 20.6 %collective-permute-start.7 = (bf16[192,1,192]{2,0,1:T(8,128)(2,1)S(1)}, bf16[192,1,192]{2,0,1:T(8,128)(2,1)S(1)}, u32[]{:S(2)}, u32[]{:S(2)}) collective-permute-start(bf16[192,1,192]{2,0,1:T(8,128)(2,1)S(1)} %get-tuple-element.168), channel_id=1, source_target_pairs={{0,8},{1,9},{2,10},{3,11},{4,12},{5,13},{6,14},{7,15},{8,0},{9,1},... | collective-permute-start | bytes 221192 | tf_op jit(solution)/shard_map/ppermute | solution.py:22
  481.9 24.9 %collective-permute-start.8 = (bf16[192,1,192]{2,0,1:T(8,128)(2,1)S(1)}, bf16[192,1,192]{2,0,1:T(8,128)(2,1)S(1)}, u32[]{:S(2)}, u32[]{:S(2)}) collective-permute-start(bf16[192,1,192]{2,0,1:T(8,128)(2,1)S(1)} %get-tuple-element.167), channel_id=1, source_target_pairs={{0,9},{1,8},{2,11},{3,10},{4,13},{5,12},{6,15},{7,14},{8,1},{9,0},... | collective-permute-start | bytes 221192 | tf_op jit(solution)/shard_map/ppermute | solution.py:22
  489.3 20.0 %collective-permute-start.9 = (bf16[192,1,192]{2,0,1:T(8,128)(2,1)S(1)}, bf16[192,1,192]{2,0,1:T(8,128)(2,1)S(1)}, u32[]{:S(2)}, u32[]{:S(2)}) collective-permute-start(bf16[192,1,192]{2,0,1:T(8,128)(2,1)S(1)} %get-tuple-element.166), channel_id=1, source_target_pairs={{0,10},{1,11},{2,8},{3,9},{4,14},{5,15},{6,12},{7,13},{8,2},{9,3},... | collective-permute-start | bytes 221192 | tf_op jit(solution)/shard_map/ppermute | solution.py:22
  491.3 75.4 %collective-permute-start.10 = (bf16[192,1,192]{2,0,1:T(8,128)(2,1)}, bf16[192,1,192]{2,0,1:T(8,128)(2,1)}, u32[]{:S(2)}, u32[]{:S(2)}) collective-permute-start(bf16[192,1,192]{2,0,1:T(8,128)(2,1)} %get-tuple-element.165), channel_id=1, source_target_pairs={{0,11},{1,10},{2,9},{3,8},{4,15},{5,14},{6,13},{7,12},{8,3},{9,2},... | collective-permute-start | bytes 221192 | tf_op jit(solution)/shard_map/ppermute | solution.py:22
  494.8 75.6 %collective-permute-start.11 = (bf16[192,1,192]{2,0,1:T(8,128)(2,1)}, bf16[192,1,192]{2,0,1:T(8,128)(2,1)}, u32[]{:S(2)}, u32[]{:S(2)}) collective-permute-start(bf16[192,1,192]{2,0,1:T(8,128)(2,1)} %get-tuple-element.164), channel_id=1, source_target_pairs={{0,12},{1,13},{2,14},{3,15},{4,8},{5,9},{6,10},{7,11},{8,4},{9,5},... | collective-permute-start | bytes 221192 | tf_op jit(solution)/shard_map/ppermute | solution.py:22
  498.7 75.5 %collective-permute-start.12 = (bf16[192,1,192]{2,0,1:T(8,128)(2,1)S(1)}, bf16[192,1,192]{2,0,1:T(8,128)(2,1)S(1)}, u32[]{:S(2)}, u32[]{:S(2)}) collective-permute-start(bf16[192,1,192]{2,0,1:T(8,128)(2,1)S(1)} %get-tuple-element.163), channel_id=1, source_target_pairs={{0,13},{1,12},{2,15},{3,14},{4,9},{5,8},{6,11},{7,10},{8,5},{9,4},... | collective-permute-start | bytes 221192 | tf_op jit(solution)/shard_map/ppermute | solution.py:22
  507.5 69.7 %collective-permute-start.13 = (bf16[192,1,192]{2,0,1:T(8,128)(2,1)S(1)}, bf16[192,1,192]{2,0,1:T(8,128)(2,1)S(1)}, u32[]{:S(2)}, u32[]{:S(2)}) collective-permute-start(bf16[192,1,192]{2,0,1:T(8,128)(2,1)S(1)} %get-tuple-element.162), channel_id=1, source_target_pairs={{0,14},{1,15},{2,12},{3,13},{4,10},{5,11},{6,8},{7,9},{8,6},{9,7},... | collective-permute-start | bytes 221192 | tf_op jit(solution)/shard_map/ppermute | solution.py:22
  509.4 3.8 copy-start.7
  509.4 70.6 %collective-permute-start.14 = (bf16[192,1,192]{2,0,1:T(8,128)(2,1)S(1)}, bf16[192,1,192]{2,0,1:T(8,128)(2,1)S(1)}, u32[]{:S(2)}, u32[]{:S(2)}) collective-permute-start(bf16[192,1,192]{2,0,1:T(8,128)(2,1)S(1)} %get-tuple-element.161), channel_id=1, source_target_pairs={{0,15},{1,14},{2,13},{3,12},{4,11},{5,10},{6,9},{7,8},{8,7},{9,6},... | collective-permute-start | bytes 221192 | tf_op jit(solution)/shard_map/ppermute | solution.py:22
  525.6 64.8 %all-to-all-start.2 = ((bf16[16,2,6144]{2,1,0:T(2,128)(2,1)}), bf16[16,2,6144]{2,1,0:T(2,128)(2,1)S(1)}, u32[]{:S(2)}, u32[]{:S(2)}) async-start(bf16[16,2,6144]{2,1,0:T(2,128)(2,1)} %reshape.337), calls=%async_computation.2 | async-start | bytes 786432 | tf_op jit(solution)/shard_map/all_to_all | solution.py:136
  546.7 14.3 %copy-start.6 = (bf16[192,1,192]{2,0,1:T(8,128)(2,1)S(1)}, bf16[192,1,192]{2,0,1:T(8,128)(2,1)}, u32[]{:S(2)}) copy-start(bf16[192,1,192]{2,0,1:T(8,128)(2,1)} %copy-done.5) | copy-start | bytes 221188
  549.6 14.3 %copy-start.8 = (bf16[192,1,192]{2,0,1:T(8,128)(2,1)S(1)}, bf16[192,1,192]{2,0,1:T(8,128)(2,1)}, u32[]{:S(2)}) copy-start(bf16[192,1,192]{2,0,1:T(8,128)(2,1)} %copy-done.7) | copy-start | bytes 221188
  (6 other events, 5.5 us)
Sparse Core Ops, SparseCore 0:
  10.2 81.2 all-gather.3
  94.5 83.6 all-gather.5
  453.0 100.2 reduce-scatter.3
